TPU v7x, 32 devices: a whole 2x2x4 slice. The times are simulated.
32 devices in a mesh: dp: 8 (over y, x, core), mp: 4 (over z).
Axes of the slice: x: 2, y: 2, z: 4, core: 2. Of those that a mesh axis runs over, the one named last changes fastest.
Arguments:
- gen_rows: bfloat16 [1024, 5120], P(('dp', 'mp')), may hold values from -6 to 6
- lengths: int32 [32, 4], P('dp'), may hold values from 1 to 16, 32 in all within a row
- assign: int32 [32, 4], P('dp'), may hold values from 0 to 3, each once within a row
- rewards: float32 [32, 4], P('dp'), may hold values from 0 to 1
- upstream: bfloat16 [2048, 2048], P('dp', 'mp'), may hold values from -6 to 6
- weight: bfloat16 [5120, 2048], P(None, 'mp'), may hold values from -0.078125 to 0.078125
- q_init: float32 [2048, 64], P('mp'), may hold values from -6 to 6
- resid: float32 [32, 128, 2048], P('dp', None, 'mp'), may hold values from -4 to 4
- block_ids: int32 [32], P('dp'), may hold values from 0 to 39, as said below
Outputs:
- p_factor: float32 [5120, 256], P(None, 'mp')
- q_factor: float32 [2048, 64], P('mp')
- resid_out: float32 [32, 128, 2048], P('dp', None, 'mp')
Inputs may be any that keep to these rules, and one draw needn't show every extreme that they name: Each row holds the lengths of one generator's 4 sequences; they sum to 32. `assign`: each row names every learner once. `block_ids`: the 4 ids of one replica are distinct.
All inputs are finite; a program needn't handle non-finite values.
Results may differ from a plain program's by a relative error of at most 0.003.
Values may be sent and summed in bfloat16 or wider, within the bound.
No kernel may reach another device: no remote copies, remote signals or barrier semaphores. Data moves between devices by JAX's collectives and lax.ppermute only.
A program may use at most 64 MiB of HBM per device.

v0:
```python
import jax
import jax.numpy as jnp
from jax import lax
from jax.sharding import PartitionSpec as P

HIGHEST_PRECISION = lax.Precision.HIGHEST


def packed_tables(lengths, assign, rewards, slot_count, capacity):
    groups, sequences = lengths.shape
    offsets = jnp.cumsum(lengths, axis=1) - lengths
    advantage = rewards - jnp.mean(rewards, axis=1, keepdims=True)
    seq_weight = advantage / lengths.astype(rewards.dtype)
    positions = jnp.arange(slot_count)
    seq_index = jnp.arange(sequences)
    inside = (offsets[:, None, :] <= positions[None, :, None]).astype(jnp.int32)
    owner = jnp.sum(inside, axis=2) - 1
    picked = owner[:, :, None] == seq_index[None, None, :]
    seq_start = jnp.sum(jnp.where(picked, offsets[:, None, :], 0), axis=2)
    learner = jnp.sum(jnp.where(picked, assign[:, None, :], 0), axis=2)
    row_weight = jnp.sum(jnp.where(picked, seq_weight[:, None, :], 0.0), axis=2)
    source = jnp.arange(groups)[:, None]
    slot_table = learner * (groups * capacity) + source * capacity + positions[None, :] - seq_start
    return (slot_table, row_weight)


def row_gradient(row_block, upstream_rows, weights_here, weight):
    hidden = jnp.dot(row_block, weight, preferred_element_type=jnp.float32)
    tangent = jnp.tanh(hidden)
    grad_h = (
        weights_here[:, None] * upstream_rows.astype(jnp.float32) * (1.0 - tangent * tangent)
    ).astype(jnp.bfloat16)
    return jnp.einsum("nd,nc->dc", row_block, grad_h, preferred_element_type=jnp.float32)


def shards(gen_rows, lengths, assign, rewards, upstream, weight, q_init, resid, block_ids):
    groups = lax.axis_size("mp")
    slot_count = gen_rows.shape[0]
    capacity = upstream.shape[0] // (groups * groups)
    slot_table, row_weight = packed_tables(lengths, assign, rewards, slot_count, capacity)
    flat_slot = slot_table.reshape(-1)
    flat_weight = row_weight.reshape(-1)
    upstream_rows = jnp.take(upstream, flat_slot, axis=0)
    gradient = row_gradient(
        lax.all_gather(gen_rows, "mp", axis=0, tiled=True), upstream_rows, flat_weight, weight
    )
    block_rows = resid.shape[1]
    for block in range(resid.shape[0]):
        first_row = block_ids[block] * block_rows
        current = lax.dynamic_slice_in_dim(gradient, first_row, block_rows, 0)
        gradient = lax.dynamic_update_slice_in_dim(gradient, current + resid[block], first_row, 0)
    p_local = jnp.dot(gradient, q_init, precision=HIGHEST_PRECISION)
    p_sum = lax.psum(p_local, "dp")
    gram_matrix = jnp.einsum("dr,ds->rs", p_sum, p_sum, precision=HIGHEST_PRECISION)
    factor_low = jnp.linalg.cholesky(gram_matrix)
    p_factor = jax.scipy.linalg.solve_triangular(factor_low, p_sum.T, lower=True).T
    q_local = jnp.einsum("dc,dr->cr", gradient, p_factor, precision=HIGHEST_PRECISION)
    q_factor = lax.psum(q_local, "dp") / lax.axis_size("dp")
    new_blocks = []
    for block in range(resid.shape[0]):
        first_row = block_ids[block] * block_rows
        merged_rows = lax.dynamic_slice_in_dim(gradient, first_row, block_rows, 0)
        p_rows = lax.dynamic_slice_in_dim(p_factor, first_row, block_rows, 0)
        approx = jnp.einsum("br,cr->bc", p_rows, q_factor, precision=HIGHEST_PRECISION)
        new_blocks.append(merged_rows - approx)
    return (p_factor, q_factor, jnp.stack(new_blocks))


def solution(mesh):
    placed = (
        P(("dp", "mp"), None),
        P("dp", None),
        P("dp", None),
        P("dp", None),
        P("dp", "mp"),
        P(None, "mp"),
        P("mp", None),
        P("dp", None, "mp"),
        P("dp"),
    )
    return jax.shard_map(
        shards,
        mesh=mesh,
        in_specs=placed,
        out_specs=(P(None, "mp"), P("mp", None), P("dp", None, "mp")),
        check_vma=False,
    )
```

profile of v0, /device:TPU:0, one launch (start us, length us, event | category | flops | bytes accessed | tf_op | source)
XLA Modules:
  0.0 227.9 jit_solution(15444329244682934595)
XLA Ops:
  7.2 0.0 all-gather.2.cloned.1.call-start
  7.2 0.7 all-gather.2.cloned.1.call-update
  7.9 0.0 all-reduce.3.cloned.1.call-start
  8.0 0.9 reduce_window_sum.11
  8.8 0.7 sub.52
  9.5 0.1 convert_reduce_fusion
  9.6 0.8 select_reduce_fusion.2
  10.4 0.1 add_subtract_fusion
  10.5 0.1 sub.58
  10.5 0.1 sub.57
  10.6 1.5 fusion.36
  14.8 0.8 reduce_sum.46
  15.6 0.8 convert_divide_fusion
  16.3 0.1 select_reduce_fusion.3
  16.4 0.1 mul.70
  16.5 1.3 fusion.35
  17.8 0.1 copy.39
  17.9 0.1 copy.38
  18.0 0.1 copy.37
  18.2 0.1 copy.36
  18.4 0.8 gather_fusion
  19.2 25.8 %all-gather.2.cloned.1.call-done = bf16[128,5120]{1,0:T(8,128)(2,1)} async-done(((bf16[32,5120]{1,0:T(8,128)(2,1)}), bf16[128,5120]{1,0:T(8,128)(2,1)}) %all-gather.2.cloned.1.call-update) | async-done | bytes 1310736 | tf_op jit(solution)/shard_map/all_gather | solution.py:45
  45.0 9.6 %fusion.8 = f32[512,5120]{1,0:T(8,128)} fusion(bf16[128,5120]{1,0:T(8,128)(2,1)} %all-gather.2.cloned.1.call-done, bf16[5120,512]{1,0:T(8,128)(2,1)} %param.14, bf16[128,512]{1,0:T(8,128)(2,1)S(1)} %gather_fusion, f32[128]{0:T(128)S(1)} %mul.70, pred[128]{0:T(512)(128)(4,1)S(1)} %compare_and_fusion), kind=kOutput, calls=%fused_computation.14 | convolution fusion | flops 1342636032 | bytes 17171072 | tf_op jit(solution)/shard_map/nd,nc->dc/dot_general | solution.py:33
  54.6 4.0 %copy.40 = f32[5120,512]{0,1:T(8,128)S(1)} copy(f32[5120,512]{0,1:T(8,128)} %bitcast.57) | data formatting | bytes 20971520
  58.7 1.0 fusion.12
  59.6 0.1 fusion.11
  59.7 0.1 fusion.10
  59.8 0.1 fusion.9
  59.9 4.0 %copy-done.1 = f32[5120,512]{0,1:T(8,128)} copy-done((f32[5120,512]{0,1:T(8,128)}, f32[5120,512]{0,1:T(8,128)S(1)}, u32[]{:S(2)}) %copy-start.1) | copy-done | bytes 10485784
  63.9 8.0 %fusion.37 = f32[5120,64]{0,1:T(8,128)} fusion(f32[5120,512]{0,1:T(8,128)S(1)} %fusion.9, f32[512,64]{0,1:T(8,128)S(1)} %copy-done.4), kind=kOutput, calls=%fused_computation.70 | convolution fusion | flops 2013265920 | bytes 11927552 | tf_op jit(solution)/shard_map/dot_general | solution.py:52
  72.0 0.2 all-reduce.5.cloned.1.call-start
  72.2 56.7 %all-reduce.3.cloned.1.call-done = f32[5120,64]{0,1:T(8,128)} async-done(((f32[5120,64]{0,1:T(8,128)}), f32[5120,64]{0,1:T(8,128)}) %all-reduce.3.cloned.1.call-update) | async-done | bytes 1310736 | tf_op jit(solution)/shard_map/psum | solution.py:53
  128.9 2.9 %fusion.38 = f32[64,64]{1,0:T(8,128)S(1)} fusion(f32[5120,64]{0,1:T(8,128)} %all-reduce.3.cloned.1.call-done), kind=kOutput, calls=%fused_computation.71 | convolution fusion | flops 251658240 | bytes 1327104 | tf_op jit(solution)/shard_map/dr,ds->rs/dot_general | solution.py:54
  131.8 0.1 copy.26
  131.9 5.8 %cholesky.16 = f32[64,64]{1,0:T(8,128)S(1)} custom-call(f32[64,64]{1,0:T(8,128)S(1)} %fusion.23), custom_call_target="Cholesky" | custom-call | tf_op jit(solution)/shard_map/jit(cholesky)/cholesky | solution.py:55
  137.7 0.6 compare_reduce_fusion
  138.4 0.7 fusion.20
  139.0 4.9 %custom-call.7 = f32[1,64,64]{1,2,0:T(8,128)S(1)} custom-call(f32[1,64,64]{2,1,0:T(8,128)S(1)} %fusion.20), custom_call_target="InvertDiagBlocksLowerTriangular" | custom-call | tf_op jit(solution)/shard_map/jit(_solve_triangular)/triangular_solve | solution.py:56
  143.9 2.6 %fusion.21 = f32[64,5120]{1,0:T(8,128)S(1)} fusion(f32[5120,64]{0,1:T(8,128)} %all-reduce.3.cloned.1.call-done, f32[1,64,64]{1,2,0:T(8,128)S(1)} %custom-call.7), kind=kOutput, calls=%fused_computation.34 | convolution fusion | flops 251658240 | bytes 2637824 | tf_op jit(solution)/shard_map/jit(_solve_triangular)/triangular_solve | solution.py:56
  146.5 13.9 %fusion.39 = f32[512,64]{0,1:T(8,128)} fusion(f32[5120,512]{0,1:T(8,128)} %copy-done.1, f32[64,5120]{1,0:T(8,128)S(1)} %fusion.21), kind=kOutput, calls=%fused_computation.72 | convolution fusion | flops 2013265920 | bytes 11927552 | tf_op jit(solution)/shard_map/dc,dr->cr/dot_general | solution.py:57
  160.5 52.3 %all-reduce.5.cloned.1.call-done = f32[512,64]{0,1:T(8,128)} async-done(((f32[512,64]{0,1:T(8,128)}), f32[512,64]{0,1:T(8,128)}) %all-reduce.5.cloned.1.call-update) | async-done | bytes 131088 | tf_op jit(solution)/shard_map/psum | solution.py:58
  212.7 0.9 broadcast_multiply_fusion
  213.7 1.6 fusion
  215.3 1.6 fusion.1
  216.8 1.6 fusion.2
  218.4 1.6 fusion.3
  220.0 0.1 pad_maximum_fusion
  220.1 1.3 copy.31
  (19 shorter events, 0.1 us)
Async XLA Ops:
  7.2 11.2 %copy-start = (bf16[256,512]{1,0:T(8,128)(2,1)S(1)}, bf16[256,512]{1,0:T(8,128)(2,1)}, u32[]{:S(2)}) copy-start(bf16[256,512]{1,0:T(8,128)(2,1)} %param.13) | copy-start | bytes 786436
  7.2 37.8 %all-gather.2.cloned.1.call-start = ((), (), s32[]{:S(2)}) async-start(), calls=%async_computation | async-start | bytes 1638400 | tf_op jit(solution)/shard_map/all_gather | solution.py:45
  7.9 120.9 %all-reduce.3.cloned.1.call-start = ((), (), s32[]{:S(2)}) async-start(), calls=%async_computation.1 | async-start | bytes 2621440 | tf_op jit(solution)/shard_map/psum | solution.py:53
  54.6 9.2 %copy-start.4 = (f32[512,64]{0,1:T(8,128)S(1)}, f32[512,64]{0,1:T(8,128)}, u32[]{:S(2)}) copy-start(f32[512,64]{0,1:T(8,128)} %param.15) | copy-start | bytes 393220
  59.9 4.0 %copy-start.1 = (f32[5120,512]{0,1:T(8,128)}, f32[5120,512]{0,1:T(8,128)S(1)}, u32[]{:S(2)}) copy-start(f32[5120,512]{0,1:T(8,128)S(1)} %fusion.9) | copy-start | bytes 31457284
  72.0 140.8 %all-reduce.5.cloned.1.call-start = ((), (), s32[]{:S(2)}) async-start(), calls=%async_computation.2 | async-start | bytes 262144 | tf_op jit(solution)/shard_map/psum | solution.py:58
  146.5 71.9 %copy-start.2 = (f32[64,5120]{1,0:T(8,128)}, f32[64,5120]{1,0:T(8,128)S(1)}, u32[]{:S(2)}) copy-start(f32[64,5120]{1,0:T(8,128)S(1)} %fusion.21) | copy-start | bytes 3932164
  213.7 7.7 %copy-start.3 = (f32[512,64]{0,1:T(8,128)}, f32[512,64]{0,1:T(8,128)S(1)}, u32[]{:S(2)}) copy-start(f32[512,64]{0,1:T(8,128)S(1)} %broadcast_multiply_fusion) | copy-start | bytes 393220
Sparse Core Ops, SparseCore 0:
  9.6 35.3 all-gather.1
  72.1 56.7 all-reduce.2
  160.6 52.1 all-reduce.4
where the time goes:
time: 228 us
  waiting for transfers between devices  135 us (59%)
  matrix products  43.3 us (19%)
  other arithmetic  18.4 us (8%)
  between operations  16.7 us (7%)
  local copies, waits for them, and re-layouts  13.7 us (6%)
    psum x1, waiting for transfers between devices, shards(): p_sum = lax.psum(p_local, 'dp')  56.7 us
    psum x1, waiting for transfers between devices, shards(): q_factor = lax.psum(q_local, 'dp') / lax.axis_size('dp')  52.3 us
    all_gather x1, waiting for transfers between devices, shards(): lax.all_gather(gen_rows, 'mp', axis=0, tiled=True)  25.8 us
    dot_general x1, matrix products, shards(): jnp.einsum('dc,dr->cr', gradient, p_factor, precision=HIGHEST_PRECISION)  13.9 us
    unnamed x16, local copies, waits for them, and re-layouts  9.83 us
    dot_general x1, matrix products, row_gradient(): jnp.einsum('nd,nc->dc', row_block, grad_h, preferred_element_type=jnp.flo...  9.64 us
    dot_general x1, matrix products, shards(): p_local = jnp.dot(gradient, q_init, precision=HIGHEST_PRECISION)  8.05 us
    another operation x3, other arithmetic, shards(): factor_low = jnp.linalg.cholesky(gram_matrix)  6.52 us
  transfers between devices with their start and end apart: 3, of which 3 were waited for; matrix products, arithmetic and copies ran while one was open for 4% of the time, Pallas kernels for 0%

commit v1 on v0

--- a/solution.py
+++ b/solution.py
@@ -4,6 +4,28 @@
 from jax.sharding import PartitionSpec as P
 
 HIGHEST_PRECISION = lax.Precision.HIGHEST
+
+
+def joined_along(blocks, dim):
+    shape = list(blocks.shape[1:])
+    shape[dim] *= blocks.shape[0]
+    return jnp.moveaxis(blocks, 0, dim).reshape(shape)
+
+
+def gather_around(x, axis, dim):
+    devices = lax.axis_size(axis)
+    pairs = [(i, (i + 1) % devices) for i in range(devices)]
+    back = [(b, a) for a, b in pairs]
+    lower, upper = ([], [])
+    for lap in range(devices - 1):
+        if lap % 2 == 0:
+            lower.append(lax.ppermute(lower[-1] if lower else x, axis, pairs))
+        else:
+            upper.append(lax.ppermute(upper[-1] if upper else x, axis, back))
+    pieces = jnp.stack([*lower[::-1], x, *upper])
+    shift = lax.axis_index(axis) - len(lower)
+    pieces = pieces[(jnp.arange(devices) - shift) % devices]
+    return joined_along(pieces, dim)
 
 
 def packed_tables(lengths, assign, rewards, slot_count, capacity):
@@ -41,9 +63,7 @@
     flat_slot = slot_table.reshape(-1)
     flat_weight = row_weight.reshape(-1)
     upstream_rows = jnp.take(upstream, flat_slot, axis=0)
-    gradient = row_gradient(
-        lax.all_gather(gen_rows, "mp", axis=0, tiled=True), upstream_rows, flat_weight, weight
-    )
+    gradient = row_gradient(gather_around(gen_rows, "mp", 0), upstream_rows, flat_weight, weight)
     block_rows = resid.shape[1]
     for block in range(resid.shape[0]):
         first_row = block_ids[block] * block_rows

time: 228 us -> 216 us (0.947)
  waiting for transfers between devices: 135 us -> 122 us
  local copies, waits for them, and re-layouts: 13.7 us -> 3.33 us
  other arithmetic: 18.4 us -> 25.2 us
  starting transfers between devices: 0.3 us -> 5.48 us
    all_gather x1 -> x0, waiting for transfers between devices: 25.8 us -> none  [shards(): lax.all_gather(gen_rows, 'mp', axis=0, tiled=True)]
    ppermute x0 -> x3, waiting for transfers between devices: none -> 12.4 us  [the longest x2 7.41 us: gather_around(): lower.append(lax.ppermute(lower[-1] if lower else x, axis, pairs))]
    unnamed x16 -> x14, local copies, waits for them, and re-layouts: 9.83 us -> 0.05 us
    dot_general x1, matrix products: 8.05 us -> 13.9 us  [shards(): p_local = jnp.dot(gradient, q_init, precision=HIGHEST_PRECISION)]
    dynamic_update_slice x4, other arithmetic: 1.2 us -> 6.82 us  [shards(): lax.dynamic_update_slice_in_dim(gradient, current + resid[block], first_r...]
    ppermute x0 -> x3, starting transfers between devices: none -> 5.23 us  [the longest x2 3.13 us: gather_around(): lower.append(lax.ppermute(lower[-1] if lower else x, axis, pairs))]
    dot_general x1, matrix products: 13.9 us -> 10.6 us  [shards(): jnp.einsum('dc,dr->cr', gradient, p_factor, precision=HIGHEST_PRECISION)]
  transfers between devices with their start and end apart: 3 -> 5, of which waited for: 3 -> 4; matrix products, arithmetic and copies ran while one was open for 4% -> 3% of each run, Pallas kernels for 0% -> 0%
where the time goes in v1:
time: 216 us
  waiting for transfers between devices  122 us (56%)
  matrix products  43.2 us (20%)
  other arithmetic  25.2 us (12%)
  between operations  16.9 us (8%)
  starting transfers between devices  5.48 us (3%)
  local copies, waits for them, and re-layouts  3.33 us (2%)
    psum x1, waiting for transfers between devices, shards(): p_sum = lax.psum(p_local, 'dp')  56.9 us
    psum x1, waiting for transfers between devices, shards(): q_factor = lax.psum(q_local, 'dp') / lax.axis_size('dp')  52.3 us
    dot_general x1, matrix products, shards(): p_local = jnp.dot(gradient, q_init, precision=HIGHEST_PRECISION)  13.9 us
    dot_general x1, matrix products, shards(): jnp.einsum('dc,dr->cr', gradient, p_factor, precision=HIGHEST_PRECISION)  10.6 us
    dot_general x1, matrix products, row_gradient(): jnp.einsum('nd,nc->dc', row_block, grad_h, preferred_element_type=jnp.flo...  8.93 us
    ppermute x2, waiting for transfers between devices, gather_around(): lower.append(lax.ppermute(lower[-1] if lower else x, axis, pairs))  7.41 us
    dynamic_update_slice x4, other arithmetic, shards(): lax.dynamic_update_slice_in_dim(gradient, current + resid[block], first_r...  6.82 us
    another operation x3, other arithmetic, shards(): factor_low = jnp.linalg.cholesky(gram_matrix)  6.52 us
  transfers between devices with their start and end apart: 5, of which 4 were waited for; matrix products, arithmetic and copies ran while one was open for 3% of the time, Pallas kernels for 0%

profile of v1, /device:TPU:0, one launch (start us, length us, event | category | flops | bytes accessed | tf_op | source)
XLA Modules:
  0.0 215.8 jit_solution(9984109470992102343)
XLA Ops:
  7.2 0.0 copy-start
  7.2 0.0 all-reduce.3.cloned.1.call-start
  7.2 3.1 %collective-permute-start = (bf16[32,5120]{1,0:T(8,128)(2,1)}, bf16[32,5120]{1,0:T(8,128)(2,1)S(1)}, u32[]{:S(2)}, u32[]{:S(2)}) collective-permute-start(bf16[32,5120]{1,0:T(8,128)(2,1)} %param.9), channel_id=1, source_target_pairs={{0,1},{1,2},{2,3},{3,0},{4,5},{5,6},{6,7},{7,4},{8,9},{9,10},{10,1... | collective-permute-start | bytes 983048 | tf_op jit(solution)/shard_map/ppermute | solution.py:22
  10.3 2.1 collective-permute-start.2
  12.4 0.9 reduce_window_sum.11
  13.3 0.7 sub.71
  13.9 0.1 convert_reduce_fusion
  14.0 0.8 select_reduce_fusion.2
  14.8 0.1 add_subtract_fusion
  14.9 0.1 sub.77
  15.0 0.1 sub.76
  15.1 1.5 fusion.37
  19.2 0.8 reduce_sum.46
  20.0 0.8 convert_divide_fusion
  20.8 0.1 select_reduce_fusion.3
  20.8 0.1 mul.70
  20.9 0.8 gather_fusion.1
  21.8 0.1 collective-permute-start.1
  21.9 5.0 %collective-permute-done.2 = bf16[32,5120]{1,0:T(8,128)(2,1)S(1)} collective-permute-done((bf16[32,5120]{1,0:T(8,128)(2,1)}, bf16[32,5120]{1,0:T(8,128)(2,1)S(1)}, u32[]{:S(2)}, u32[]{:S(2)}) %collective-permute-start.2) | collective-permute-done | bytes 327712 | tf_op jit(solution)/shard_map/ppermute | solution.py:24
  26.9 7.4 %collective-permute-done.1 = bf16[32,5120]{1,0:T(8,128)(2,1)S(1)} collective-permute-done((bf16[32,5120]{1,0:T(8,128)(2,1)S(1)}, bf16[32,5120]{1,0:T(8,128)(2,1)S(1)}, u32[]{:S(2)}, u32[]{:S(2)}) %collective-permute-start.1) | collective-permute-done | bytes 327712 | tf_op jit(solution)/shard_map/ppermute | solution.py:22
  34.3 0.2 pad_maximum_fusion
  34.5 0.6 gather_fusion
  35.2 8.9 %fusion.8 = f32[5120,512]{1,0:T(8,128)} fusion(bf16[128,5120]{1,0:T(8,128)(2,1)S(1)} %bitcast.61, bf16[5120,512]{1,0:T(8,128)(2,1)} %param.14, bf16[128,512]{1,0:T(8,128)(2,1)S(1)} %gather_fusion.1, f32[128]{0:T(128)S(1)} %mul.70, pred[128]{0:T(512)(128)(4,1)S(1)} %compare_and_fusion), kind=kOutput, calls=%fused_computation.16 | convolution fusion | flops 1342636032 | bytes 17171072 | tf_op jit(solution)/shard_map/nd,nc->dc/dot_general | solution.py:55
  44.1 1.7 fusion.12
  45.8 1.7 fusion.11
  47.5 1.7 fusion.10
  49.2 1.7 fusion.9
  50.9 13.9 %fusion.38 = f32[5120,64]{0,1:T(8,128)} fusion(f32[5120,512]{1,0:T(8,128)} %fusion.9, f32[512,64]{0,1:T(8,128)S(1)} %copy-done.6), kind=kOutput, calls=%fused_computation.78 | convolution fusion | flops 2013265920 | bytes 11927552 | tf_op jit(solution)/shard_map/dot_general | solution.py:72
  64.8 0.0 all-reduce.3.cloned.1.call-update
  64.8 0.2 all-reduce.5.cloned.1.call-start
  65.1 56.9 %all-reduce.3.cloned.1.call-done = f32[5120,64]{0,1:T(8,128)} async-done(((f32[5120,64]{0,1:T(8,128)}), f32[5120,64]{0,1:T(8,128)}) %all-reduce.3.cloned.1.call-update) | async-done | bytes 1310736 | tf_op jit(solution)/shard_map/psum | solution.py:73
  122.0 3.0 %fusion.39 = f32[64,64]{1,0:T(8,128)S(1)} fusion(f32[5120,64]{0,1:T(8,128)} %all-reduce.3.cloned.1.call-done), kind=kOutput, calls=%fused_computation.79 | convolution fusion | flops 251658240 | bytes 1327104 | tf_op jit(solution)/shard_map/dr,ds->rs/dot_general | solution.py:74
  125.0 0.1 copy.13
  125.1 5.8 %cholesky.16 = f32[64,64]{1,0:T(8,128)S(1)} custom-call(f32[64,64]{1,0:T(8,128)S(1)} %fusion.23), custom_call_target="Cholesky" | custom-call | tf_op jit(solution)/shard_map/jit(cholesky)/cholesky | solution.py:75
  131.0 0.6 compare_reduce_fusion
  131.7 0.7 fusion.20
  132.3 4.9 %custom-call.7 = f32[1,64,64]{1,2,0:T(8,128)S(1)} custom-call(f32[1,64,64]{2,1,0:T(8,128)S(1)} %fusion.20), custom_call_target="InvertDiagBlocksLowerTriangular" | custom-call | tf_op jit(solution)/shard_map/jit(_solve_triangular)/triangular_solve | solution.py:76
  137.2 0.0 copy-done.1
  137.2 1.2 fusion.21
  138.5 10.6 %fusion.40 = f32[512,64]{0,1:T(8,128)} fusion(f32[5120,512]{1,0:T(8,128)} %fusion.9, f32[64,5120]{1,0:T(8,128)S(1)} %fusion.21), kind=kOutput, calls=%fused_computation.80 | convolution fusion | flops 2013265920 | bytes 11927552 | tf_op jit(solution)/shard_map/dc,dr->cr/dot_general | solution.py:77
  149.1 0.0 all-reduce.5.cloned.1.call-update
  149.1 52.3 %all-reduce.5.cloned.1.call-done = f32[512,64]{0,1:T(8,128)} async-done(((f32[512,64]{0,1:T(8,128)}), f32[512,64]{0,1:T(8,128)}) %all-reduce.5.cloned.1.call-update) | async-done | bytes 131088 | tf_op jit(solution)/shard_map/psum | solution.py:78
  201.4 0.9 broadcast_multiply_fusion
  202.3 1.4 fusion
  203.8 1.4 fusion.1
  205.2 1.4 fusion.2
  206.6 1.4 fusion.3
  207.9 1.0 pad_maximum_fusion.1
  (23 shorter events, 0.1 us)
Async XLA Ops:
  7.2 13.8 %copy-start = (bf16[256,512]{1,0:T(8,128)(2,1)S(1)}, bf16[256,512]{1,0:T(8,128)(2,1)}, u32[]{:S(2)}) copy-start(bf16[256,512]{1,0:T(8,128)(2,1)} %param.13) | copy-start | bytes 786436
  7.2 27.2 %copy-start.5 = (bf16[32,5120]{1,0:T(8,128)(2,1)S(1)}, bf16[32,5120]{1,0:T(8,128)(2,1)}, u32[]{:S(2)}) copy-start(bf16[32,5120]{1,0:T(8,128)(2,1)} %param.9) | copy-start | bytes 983044
  7.2 114.8 %all-reduce.3.cloned.1.call-start = ((), (), s32[]{:S(2)}) async-start(), calls=%async_computation | async-start | bytes 2621440 | tf_op jit(solution)/shard_map/psum | solution.py:73
  7.2 14.6 %collective-permute-start = (bf16[32,5120]{1,0:T(8,128)(2,1)}, bf16[32,5120]{1,0:T(8,128)(2,1)S(1)}, u32[]{:S(2)}, u32[]{:S(2)}) collective-permute-start(bf16[32,5120]{1,0:T(8,128)(2,1)} %param.9), channel_id=1, source_target_pairs={{0,1},{1,2},{2,3},{3,0},{4,5},{5,6},{6,7},{7,4},{8,9},{9,10},{10,1... | collective-permute-start | bytes 983048 | tf_op jit(solution)/shard_map/ppermute | solution.py:22
  10.3 16.6 %collective-permute-start.2 = (bf16[32,5120]{1,0:T(8,128)(2,1)}, bf16[32,5120]{1,0:T(8,128)(2,1)S(1)}, u32[]{:S(2)}, u32[]{:S(2)}) collective-permute-start(bf16[32,5120]{1,0:T(8,128)(2,1)} %param.9), channel_id=1, source_target_pairs={{1,0},{2,1},{3,2},{0,3},{5,4},{6,5},{7,6},{4,7},{9,8},{10,9},{11,1... | collective-permute-start | bytes 983048 | tf_op jit(solution)/shard_map/ppermute | solution.py:24
  21.8 12.5 %collective-permute-start.1 = (bf16[32,5120]{1,0:T(8,128)(2,1)S(1)}, bf16[32,5120]{1,0:T(8,128)(2,1)S(1)}, u32[]{:S(2)}, u32[]{:S(2)}) collective-permute-start(bf16[32,5120]{1,0:T(8,128)(2,1)S(1)} %collective-permute-done), channel_id=1, source_target_pairs={{0,1},{1,2},{2,3},{3,0},{4,5},{5,6},{6,7},{7,4},{8,9},{9,10},{10,1... | collective-permute-start | bytes 983048 | tf_op jit(solution)/shard_map/ppermute | solution.py:22
  35.2 8.9 %copy-start.4 = (f32[4,128,512]{2,1,0:T(8,128)S(1)}, f32[4,128,512]{2,1,0:T(8,128)}, u32[]{:S(2)}) copy-start(f32[4,128,512]{2,1,0:T(8,128)} %param.16) | copy-start | bytes 3145732
  45.8 5.1 %copy-start.6 = (f32[512,64]{0,1:T(8,128)S(1)}, f32[512,64]{0,1:T(8,128)}, u32[]{:S(2)}) copy-start(f32[512,64]{0,1:T(8,128)} %param.15) | copy-start | bytes 393220
  64.8 136.6 %all-reduce.5.cloned.1.call-start = ((), (), s32[]{:S(2)}) async-start(), calls=%async_computation.1 | async-start | bytes 262144 | tf_op jit(solution)/shard_map/psum | solution.py:78
  122.0 15.2 %copy-start.1 = (f32[5120,64]{0,1:T(8,128)S(1)}, f32[5120,64]{0,1:T(8,128)}, u32[]{:S(2)}) copy-start(f32[5120,64]{0,1:T(8,128)} %all-reduce.3.cloned.1.call-done) | copy-start | bytes 3932164
  138.5 68.1 %copy-start.2 = (f32[64,5120]{1,0:T(8,128)}, f32[64,5120]{1,0:T(8,128)S(1)}, u32[]{:S(2)}) copy-start(f32[64,5120]{1,0:T(8,128)S(1)} %fusion.21) | copy-start | bytes 3932164
  202.3 5.6 %copy-start.3 = (f32[512,64]{0,1:T(8,128)}, f32[512,64]{0,1:T(8,128)S(1)}, u32[]{:S(2)}) copy-start(f32[512,64]{0,1:T(8,128)S(1)} %broadcast_multiply_fusion) | copy-start | bytes 393220
Sparse Core Ops, SparseCore 0:
  65.0 57.0 all-reduce.2
  149.2 52.1 all-reduce.4
